TPU v7x, 128 devices: a whole 4x4x4 slice. The times are simulated.
128 devices in a mesh: src: 8 (over y, z_lo), rcv: 16 (over x, z_hi, core).
Axes of the slice: x: 4, y: 4, z: 4 (z_hi: 2, z_lo: 2; z = z_hi * 2 + z_lo), core: 2. Of those that a mesh axis runs over, the one named last changes fastest.
Arguments:
- traces: float32 [512, 512, 1024], P('src', 'rcv'), may hold values from -6 to 6
- freq_index: int32 [256], replicated, may hold values from 1 to 511, as said below
- primaries: float32 [256, 2, 512, 512], P(('src', 'rcv')), may hold values from -0.1875 to 0.1875
Outputs:
- residual: float32 [256, 2, 512, 512], P(('src', 'rcv'))
- residual_next: float32 [256, 2, 512, 512], P(('src', 'rcv'))
Inputs may be any that keep to these rules, and one draw needn't show every extreme that they name: `freq_index`: sorted ascending; repeats possible; the first is 1 and the last is 511.
All inputs are finite; a program needn't handle non-finite values.
Results may differ from a plain program's by a relative error of at most 0.00012.
Values sent between devices are 32-bit elements; how exact they have to be, the bound alone decides.
A program may use at most 128 MiB of HBM per device.

v0:
```python
import math

import jax
import jax.numpy as jnp
from jax import lax
from jax.sharding import PartitionSpec as P


def freq_table(freq_index, samples):
    times = jnp.arange(samples, dtype=jnp.int32)
    phase = freq_index[:, None] * times[None, :] % samples
    angle = phase.astype(jnp.float32) * (2.0 * math.pi / samples)
    return jnp.stack([jnp.cos(angle), -jnp.sin(angle)], axis=1) / math.sqrt(samples)


def matrix_product(left, right):
    return jnp.einsum("fij,fjk->fik", left, right, precision=lax.Precision.HIGHEST)


def complex_product(left_re, left_im, right_re, right_im, adjoint):
    if adjoint:
        right_re = jnp.swapaxes(right_re, 1, 2)
        right_im = -jnp.swapaxes(right_im, 1, 2)
    real_part = matrix_product(left_re, right_re) - matrix_product(left_im, right_im)
    imag_part = matrix_product(left_re, right_im) + matrix_product(left_im, right_re)
    return (real_part, imag_part)


def on_device(traces, freq_index, primaries):
    src_local, rcv_local, samples = traces.shape
    n_src = lax.axis_size("src")
    n_rcv = lax.axis_size("rcv")
    table = freq_table(freq_index, samples)
    flat = traces.reshape(src_local * rcv_local, samples)
    spectrum = lax.dot_general(
        table,
        flat,
        (((2,), (1,)), ((), ())),
        precision=lax.Precision.HIGHEST,
        preferred_element_type=jnp.float32,
    )
    spectrum = spectrum[None]
    freq_local = primaries.shape[0]
    arrived = lax.all_to_all(spectrum, ("src", "rcv"), split_axis=1, concat_axis=0, tiled=True)
    arrived = arrived.reshape(n_src, n_rcv, freq_local, 2, src_local, rcv_local)
    arrived = jnp.transpose(arrived, (2, 3, 0, 4, 1, 5))
    whole = arrived.reshape(freq_local, 2, n_src * src_local, n_rcv * rcv_local)
    data_re = 0.5 * (whole[:, 0] + jnp.swapaxes(whole[:, 0], 1, 2))
    data_im = 0.5 * (whole[:, 1] + jnp.swapaxes(whole[:, 1], 1, 2))
    model_re, model_im = complex_product(primaries[:, 0], primaries[:, 1], data_re, data_im, False)
    resid_re = data_re - model_re
    resid_im = data_im - model_im
    grad_re, grad_im = complex_product(resid_re, resid_im, data_re, data_im, True)
    pred_re, pred_im = complex_product(grad_re, grad_im, data_re, data_im, False)
    offset = (lax.axis_index("src") * n_rcv + lax.axis_index("rcv")) * freq_local
    weights = freq_index.astype(jnp.float32) / (samples // 2)
    weights = lax.dynamic_slice_in_dim(weights, offset, freq_local)
    scaled = weights[:, None, None]
    numer = jnp.sum(scaled * (resid_re * pred_re + resid_im * pred_im))
    denom = jnp.sum(scaled * (pred_re * pred_re + pred_im * pred_im))
    numer, denom = lax.psum((numer, denom), ("src", "rcv"))
    step_size = numer / denom
    resid = jnp.stack([resid_re, resid_im], 1)
    pred = jnp.stack([pred_re, pred_im], 1)
    return (resid, resid - step_size * pred)


def solution(mesh):
    in_specs = (P("src", "rcv", None), P(), P(("src", "rcv"), None, None, None))
    out_specs = (P(("src", "rcv"), None, None, None), P(("src", "rcv"), None, None, None))
    return jax.shard_map(
        on_device, mesh=mesh, in_specs=in_specs, out_specs=out_specs, check_vma=False
    )
```

profile of v0, /device:TPU:1, one launch (start us, length us, event | category | flops | bytes accessed | tf_op | source)
XLA Modules:
  0.0 274.0 jit_solution(13504131012226300293)
XLA Ops:
  0.6 4.9 %fusion.38 = (f32[256,1,1024]{2,0,1:T(8,128)S(1)}, f32[256,1,1024]{2,0,1:T(8,128)S(1)}) fusion(s32[256]{0:T(256)} %param.4), kind=kLoop, calls=%fused_computation.46 | loop fusion | flops 3932160 | bytes 2098176 | tf_op jit(solution)/shard_map/cos | solution.py:13
  5.5 16.4 %convolution_bitcast_fusion = f32[1,256,2,2048]{3,1,2,0:T(8,128)S(1)} fusion(f32[2048,1024,1]{1,0,2:T(8,128)} %bitcast.79, f32[256,1,1024]{2,0,1:T(8,128)S(1)} %get-tuple-element.19, f32[256,1,1024]{2,0,1:T(8,128)S(1)} %get-tuple-element.18), kind=kOutput, calls=%fused_computation.3 | convolution fusion | flops 12885950464 | bytes 14680064 | tf_op jit(solution)/shard_map/dot_general | solution.py:35
  21.9 5.2 %copy.54 = f32[1,256,2,2048]{3,2,0,1:T(2,128)} copy(f32[1,256,2,2048]{3,1,2,0:T(8,128)S(1)} %convolution_bitcast_fusion) | data formatting | bytes 8388608 | tf_op jit(solution)/shard_map/broadcast_in_dim | solution.py:42
  27.2 12.7 %all-to-all-start = ((f32[1,256,2,2048]{3,2,0,1:T(2,128)}), f32[1,256,2,2048]{3,2,0,1:T(2,128)}, u32[]{:S(2)}, u32[]{:S(2)}) async-start(f32[1,256,2,2048]{3,2,0,1:T(2,128)} %copy.54), calls=%async_computation | async-start | bytes 8388608 | tf_op jit(solution)/shard_map/all_to_all | solution.py:44
  40.0 51.5 %all-to-all-done = f32[1,256,2,2048]{3,2,0,1:T(2,128)} async-done(((f32[1,256,2,2048]{3,2,0,1:T(2,128)}), f32[1,256,2,2048]{3,2,0,1:T(2,128)}, u32[]{:S(2)}, u32[]{:S(2)}) %all-to-all-start) | async-done | bytes 4194336 | tf_op jit(solution)/shard_map/all_to_all | solution.py:44
  91.4 6.6 %copy.55 = f32[1,256,2,2048]{3,1,2,0:T(8,128)} copy(f32[1,256,2,2048]{3,2,0,1:T(2,128)} %all-to-all-done) | data formatting | bytes 8388608 | tf_op jit(solution)/shard_map/all_to_all | solution.py:44
  98.1 11.4 %reshape.113 = f32[8,16,2,2,64,32]{5,4,2,1,0,3:T(8,128)} reshape(f32[1,256,2,2048]{3,1,2,0:T(8,128)} %copy.55) | data formatting | bytes 8388608 | tf_op jit(solution)/shard_map/reshape | solution.py:45
  109.5 12.8 %copy.56 = f32[2,2,8,64,16,32]{3,2,5,4,1,0:T(8,128)} copy(f32[2,2,8,64,16,32]{5,3,0,4,2,1:T(8,128)} %bitcast.75) | data formatting | bytes 8388608 | tf_op jit(solution)/shard_map/transpose | solution.py:46
  122.2 7.5 %reshape.114 = f32[2,2,512,512]{2,3,1,0:T(8,128)} reshape(f32[2,2,8,64,16,32]{3,2,5,4,1,0:T(8,128)} %copy.56) | data formatting | bytes 8388608 | tf_op jit(solution)/shard_map/reshape | solution.py:47
  129.7 4.7 %fusion.41 = (f32[2,1,512,512]{2,3,1,0:T(8,128)}, f32[2,1,512,512]{2,3,1,0:T(8,128)}) fusion(f32[2,2,512,512]{2,3,1,0:T(8,128)} %reshape.114), kind=kLoop, calls=%fused_computation.50 | loop fusion | bytes 8388608 | tf_op jit(solution)/shard_map/slice | solution.py:48
  139.2 4.1 %fusion.12 = (f32[2,512,512]{1,2,0:T(8,128)S(1)}, f32[2,512,512]{1,2,0:T(8,128)S(1)}) fusion(f32[2,1,512,512]{3,2,0,1:T(8,128)S(1)} %copy.97, f32[2,2,512,512]{2,3,1,0:T(8,128)} %reshape.114, f32[2,1,512,512]{3,2,0,1:T(8,128)} %copy.99), kind=kLoop, calls=%fused_computation.18 | loop fusion | flops 2097152 | bytes 12582912 | tf_op jit(solution)/shard_map/mul | solution.py:48
  150.4 3.9 %bitcast_subtract_fusion.1 = f32[2,512,512]{1,2,0:T(8,128)S(1)} fusion(f32[2,512,512]{1,2,0:T(8,128)S(1)} %get-tuple-element.14, f32[2,512,512]{2,1,0:T(8,128)S(1)} %fusion.5, f32[2,2,512,512]{3,2,1,0:T(8,128)S(1)} %copy-done.2), kind=kOutput, calls=%fused_computation.20 | convolution fusion | flops 3222274048 | bytes 10485760 | tf_op jit(solution)/shard_map/fij,fjk->fik/dot_general | solution.py:17
  157.8 3.8 %bitcast_subtract_fusion = f32[2,512,512]{1,2,0:T(8,128)S(1)} fusion(f32[2,512,512]{1,2,0:T(8,128)S(1)} %get-tuple-element.15, f32[2,512,512]{2,1,0:T(8,128)S(1)} %fusion.3, f32[2,2,512,512]{3,2,1,0:T(8,128)S(1)} %copy-done.2), kind=kOutput, calls=%fused_computation.19 | convolution fusion | flops 3222274048 | bytes 10485760 | tf_op jit(solution)/shard_map/fij,fjk->fik/dot_general | solution.py:17
  161.6 3.7 %fusion.44 = f32[2,512,512]{2,1,0:T(8,128)S(1)} fusion(f32[2,512,512]{1,2,0:T(8,128)S(1)} %bitcast_subtract_fusion, f32[2,512,512]{1,2,0:T(8,128)S(1)} %get-tuple-element.14), kind=kOutput, calls=%fused_computation.53 | convolution fusion | flops 3221225472 | bytes 6291456 | tf_op jit(solution)/shard_map/fij,fjk->fik/dot_general | solution.py:17
  165.3 3.9 %fusion.25 = f32[2,512,512]{2,1,0:T(8,128)S(1)} fusion(f32[2,512,512]{2,1,0:T(8,128)S(1)} %fusion.42, f32[2,512,512]{1,2,0:T(8,128)S(1)} %bitcast_subtract_fusion, f32[2,512,512]{1,2,0:T(8,128)S(1)} %get-tuple-element.15), kind=kOutput, calls=%fused_computation.31 | convolution fusion | flops 3222274048 | bytes 8388608 | tf_op jit(solution)/shard_map/fij,fjk->fik/dot_general | solution.py:17
  169.3 3.6 %fusion.45 = f32[2,512,512]{1,2,0:T(8,128)S(1)} fusion(f32[2,512,512]{2,1,0:T(8,128)S(1)} %fusion.25, f32[2,512,512]{1,2,0:T(8,128)S(1)} %get-tuple-element.15), kind=kOutput, calls=%fused_computation.54 | convolution fusion | flops 3221225472 | bytes 6291456 | tf_op jit(solution)/shard_map/fij,fjk->fik/dot_general | solution.py:17
  172.9 3.6 %fusion.43 = f32[2,512,512]{1,2,0:T(8,128)S(1)} fusion(f32[2,512,512]{2,1,0:T(8,128)S(1)} %fusion.25, f32[2,512,512]{1,2,0:T(8,128)S(1)} %get-tuple-element.14), kind=kOutput, calls=%fused_computation.52 | convolution fusion | flops 3221225472 | bytes 6291456 | tf_op jit(solution)/shard_map/fij,fjk->fik/dot_general | solution.py:17
  176.5 4.0 %fusion.28 = f32[2,512,512]{2,1,0:T(8,128)S(1)} fusion(f32[2,512,512]{2,1,0:T(8,128)S(1)} %fusion.44, f32[2,512,512]{1,2,0:T(8,128)S(1)} %bitcast_subtract_fusion.1, f32[2,512,512]{1,2,0:T(8,128)S(1)} %get-tuple-element.15), kind=kOutput, calls=%fused_computation.32 | convolution fusion | flops 3222274048 | bytes 8388608 | tf_op jit(solution)/shard_map/fij,fjk->fik/dot_general | solution.py:17
  180.5 3.6 %convolution_subtract_fusion = f32[2,512,512]{1,2,0:T(8,128)S(1)} fusion(f32[2,512,512]{1,2,0:T(8,128)S(1)} %fusion.43, f32[2,512,512]{2,1,0:T(8,128)S(1)} %fusion.28, f32[2,512,512]{1,2,0:T(8,128)S(1)} %get-tuple-element.15), kind=kOutput, calls=%fused_computation.34 | convolution fusion | flops 3221749760 | bytes 8388608 | tf_op jit(solution)/shard_map/fij,fjk->fik/dot_general | solution.py:17
  184.1 6.2 %multiply_reduce_fusion = (f32[]{:T(128)}, f32[]{:T(128)}, f32[2,512,512]{1,2,0:T(8,128)}) fusion(f32[2,512,512]{1,2,0:T(8,128)S(1)} %convolution_subtract_fusion, f32[2]{0:T(128)S(1)} %dynamic_slice.3, f32[2,512,512]{1,2,0:T(8,128)S(1)} %bitcast_subtract_fusion, f32[2,512,512]{1,2,0:T(8,128)S(1)} %bitcast_subtract_fusion.1, ...), kind=kOutput, calls=%fused_computation.21 | convolution fusion | flops 3226992640 | bytes 14680080 | tf_op jit(solution)/shard_map/fij,fjk->fik/dot_general | solution.py:17
  190.4 63.8 %all-reduce = (f32[]{:T(128)}, f32[]{:T(128)}) all-reduce(f32[]{:T(128)} %get-tuple-element.9, f32[]{:T(128)} %get-tuple-element.8), channel_id=1, replica_groups=mesh['src'=8,'rcv'=16] {'src','rcv'}, use_global_device_ids=true, to_apply=%region_1.2 | all-reduce | flops 2 | bytes 16 | tf_op jit(solution)/shard_map/psum | solution.py:61
  255.5 7.8 %fusion = (f32[2,2,512,512]{2,3,0,1:T(8,128)}, f32[2,2,512,512]{2,3,0,1:T(8,128)}) fusion(f32[2,1,512,512]{2,3,0,1:T(8,128)} %bitcast.80, f32[2,1,512,512]{2,3,0,1:T(8,128)} %bitcast.78, f32[]{:T(128)S(6)} %div.19, f32[2,1,512,512]{2,3,0,1:T(8,128)} %bitcast.77, f32[2,1,512,512]{2,3,0,1:T(8,128)S(1)} %bitcast.76), kind=kLoop, calls=%fused_computation.2 | loop fusion | flops 4194304 | bytes 16777220 | tf_op jit(solution)/shard_map/sub | solution.py:65
  263.4 5.2 %copy.79 = f32[2,2,512,512]{3,2,1,0:T(8,128)} copy(f32[2,2,512,512]{2,3,0,1:T(8,128)} %get-tuple-element.13) | data formatting | bytes 8388608
  268.6 5.2 %copy.80 = f32[2,2,512,512]{3,2,1,0:T(8,128)} copy(f32[2,2,512,512]{2,3,0,1:T(8,128)} %get-tuple-element.12) | data formatting | bytes 8388608
  (15 shorter events, 15.5 us)
Async XLA Ops:
  27.2 12.7 %copy-start.3 = (s32[256]{0:T(256)S(1)}, s32[256]{0:T(256)}, u32[]{:S(2)}) copy-start(s32[256]{0:T(256)} %param.4) | copy-start | bytes 3076
  27.2 64.3 %all-to-all-start = ((f32[1,256,2,2048]{3,2,0,1:T(2,128)}), f32[1,256,2,2048]{3,2,0,1:T(2,128)}, u32[]{:S(2)}, u32[]{:S(2)}) async-start(f32[1,256,2,2048]{3,2,0,1:T(2,128)} %copy.54), calls=%async_computation | async-start | bytes 8388608 | tf_op jit(solution)/shard_map/all_to_all | solution.py:44
  139.2 4.1 %copy-start.2 = (f32[2,2,512,512]{3,2,1,0:T(8,128)S(1)}, f32[2,2,512,512]{3,2,1,0:T(8,128)}, u32[]{:S(2)}) copy-start(f32[2,2,512,512]{3,2,1,0:T(8,128)} %param.5) | copy-start | bytes 12582916
  161.6 22.5 %copy-start = (f32[2,512,512]{1,2,0:T(8,128)}, f32[2,512,512]{1,2,0:T(8,128)S(1)}, u32[]{:S(2)}) copy-start(f32[2,512,512]{1,2,0:T(8,128)S(1)} %bitcast_subtract_fusion) | copy-start | bytes 6291460
  184.1 6.3 %copy-start.1 = (f32[2,512,512]{1,2,0:T(8,128)}, f32[2,512,512]{1,2,0:T(8,128)S(1)}, u32[]{:S(2)}) copy-start(f32[2,512,512]{1,2,0:T(8,128)S(1)} %convolution_subtract_fusion) | copy-start | bytes 6291460
where the time goes:
time: 279 us; the launch traced here: 274 us
  blocking collectives  63.8 us (23%)
  local copies, waits for them, and re-layouts  63.5 us (23%)
  matrix products  63.4 us (23%)
  waiting for transfers between devices  51.5 us (18%)
  other arithmetic  16.8 us (6%)
  starting transfers between devices  12.7 us (5%)
    psum x1, blocking collectives, on_device(): numer, denom = lax.psum((numer, denom), ('src', 'rcv'))  63.8 us
    all_to_all x1, waiting for transfers between devices, on_device(): lax.all_to_all(spectrum, ('src', 'rcv'), split_axis=1, concat_axis=0, til...  51.5 us
    dot_general x12, matrix products, matrix_product(): jnp.einsum('fij,fjk->fik', left, right, precision=lax.Precision.HIGHEST)  47 us
    dot_general x1, matrix products, on_device(): lax.dot_general(table, flat, (((2,), (1,)), ((), ())), precision=lax.Prec...  16.4 us
    unnamed x12, local copies, waits for them, and re-layouts  15.3 us
    transpose x1, local copies, waits for them, and re-layouts, on_device(): arrived = jnp.transpose(arrived, (2, 3, 0, 4, 1, 5))  12.8 us
    all_to_all x1, starting transfers between devices, on_device(): lax.all_to_all(spectrum, ('src', 'rcv'), split_axis=1, concat_axis=0, til...  12.7 us
    reshape x1, local copies, waits for them, and re-layouts, on_device(): arrived = arrived.reshape(n_src, n_rcv, freq_local, 2, src_local, rcv_local)  11.4 us
  transfers between devices with their start and end apart: 1, of which 1 were waited for; matrix products, arithmetic and copies ran while one was open for 0% of the time, Pallas kernels for 0%

commit v1 on v0

v1 whole, which is shorter than its diff:
```python
import math
import random

import jax
import jax.numpy as jnp
from jax import lax
from jax.experimental import pallas as pl
from jax.experimental.pallas import tpu as pltpu
from jax.sharding import PartitionSpec as P

MESH = pl.DeviceIdType.MESH
F32, BF16 = jnp.float32, jnp.bfloat16
NN = (((1,), (0,)), ((), ()))
NT = (((1,), (1,)), ((), ()))
N = 512
DEVICES = 128


def displacements():
    every = [(x, y, z, c) for x in range(4) for y in range(4) for z in range(4) for c in range(2)]
    every = every[1:]
    random.Random(0).shuffle(every)
    return every


def halves(x):
    high = x.astype(BF16)
    return high, (x - high.astype(F32)).astype(BF16)


def dot3(left, right, dims=NN):
    def one(a, b):
        return lax.dot_general(a, b, dims, preferred_element_type=F32)

    return one(left[0], right[0]) + (one(left[0], right[1]) + one(left[1], right[0]))


def cos_sin(steps):
    quarter = (steps + 128) >> 8
    angle = (steps - quarter * 256).astype(F32) * (2.0 * math.pi / 1024)
    square = angle * angle
    cos = 1.0 / 40320 - square * (1.0 / 3628800)
    for term in (-1.0 / 720, 1.0 / 24, -0.5, 1.0):
        cos = term + square * cos
    sin = -1.0 / 5040 + square * (1.0 / 362880)
    for term in (1.0 / 120, -1.0 / 6, 1.0):
        sin = term + square * sin
    sin = angle * sin
    quarter = quarter & 3
    odd = (quarter & 1) == 1
    cos, sin = jnp.where(odd, sin, cos), jnp.where(odd, cos, sin)
    cos = jnp.where((quarter == 1) | (quarter == 2), -cos, cos)
    sin = jnp.where(quarter >= 2, -sin, sin)
    return cos, sin


def kernel(
    traces_ref, freq_ref, weight_ref, prim_ref,
    resid_out, pred_out, step_out,
    raw, xh, xl, th, tl, sbuf, rbuf, prim, ah, al, whole, dh, dl, rh, rl, hh, hl, resid, pred, stat, slots,
    raw_sem, prim_sem, send_sem, recv_sem, own_sem, out_sem, stat_send, stat_recv,
):
    src, rcv = lax.axis_index("src"), lax.axis_index("rcv")
    me = src * 16 + rcv
    xs = [(rcv // 4 + d) % 4 for d in range(4)]
    ys = [(src // 2 + d) % 4 for d in range(4)]
    zs = [((rcv // 2) % 2 * 2 + src % 2 + d) % 4 for d in range(4)]
    cores = [(rcv + d) % 2 for d in range(2)]
    src_of = [[ys[y] * 2 + zs[z] % 2 for z in range(4)] for y in range(4)]
    rcv_of = [[[xs[x] * 4 + zs[z] // 2 * 2 + cores[c] for c in range(2)] for z in range(4)] for x in range(4)]
    order = displacements()

    def target(disp):
        x, y, z, c = disp
        return src_of[y][z], rcv_of[x][z][c]

    def load(b, g):
        return pltpu.make_async_copy(traces_ref.at[g, pl.ds(b * 4, 4)], raw.at[b, :, g], raw_sem.at[b])

    for b in range(4):
        for g in range(4):
            load(b, g).start()
    prim_copy = pltpu.make_async_copy(prim_ref, prim, prim_sem)
    prim_copy.start()

    barrier = pltpu.get_barrier_semaphore()
    for disp in order:
        pl.semaphore_signal(barrier, inc=1, device_id=target(disp), device_id_type=MESH)

    lane = lax.broadcasted_iota(jnp.int32, (128, 128), 1)
    for j in range(2):
        freq = freq_ref[pl.ds(j * 128, 128), :]
        cos, sin = cos_sin((freq * lane) & 1023)
        cos, sin = cos * 0.03125, sin * 0.03125
        turn_cos, turn_sin = cos_sin((freq * 128) & 1023)
        sign = 1.0 - 2.0 * (freq & 1).astype(F32)
        for a in range(4):
            if a:
                cos, sin = cos * turn_cos - sin * turn_sin, sin * turn_cos + cos * turn_sin
            for c, part in enumerate((cos, -sin)):
                for k, value in ((a, part), (a + 4, part * sign)):
                    high, low = halves(value)
                    th[j, c * 128 : c * 128 + 128, k * 128 : k * 128 + 128] = high
                    tl[j, c * 128 : c * 128 + 128, k * 128 : k * 128 + 128] = low

    def transform(j, b):
        rows = pl.ds(pl.multiple_of(b * 512, 512), 512)
        out = dot3((th[j], tl[j]), (xh[rows, :], xl[rows, :]), NT)
        for c in range(2):
            for d in range(0, 128, 8):
                for i in range(4):
                    start = j * DEVICES * 32 + d * 32 + c * 16 + b * 4 + i
                    sbuf[pl.ds(start, 8, stride=32), :] = out[
                        c * 128 + d : c * 128 + d + 8, i * 128 : i * 128 + 128
                    ]

    def piece(j, index):
        return pl.ds(pl.multiple_of((j * DEVICES + index) * 32, 32), 32)

    def remote(j, disp):
        to_src, to_rcv = target(disp)
        return pltpu.make_async_remote_copy(
            src_ref=sbuf.at[piece(j, to_src * 16 + to_rcv)],
            dst_ref=rbuf.at[piece(j, me)],
            send_sem=send_sem.at[j],
            recv_sem=recv_sem.at[j],
            device_id=(to_src, to_rcv),
            device_id_type=MESH,
        )

    def own(j):
        return pltpu.make_async_copy(sbuf.at[piece(j, me)], rbuf.at[piece(j, me)], own_sem.at[j])

    @pl.loop(0, 4)
    def _(b):
        for g in range(4):
            load(b, g).wait()
        high, low = halves(raw[b].reshape(512, 1024))
        rows = pl.ds(pl.multiple_of(b * 512, 512), 512)
        xh[rows, :] = high
        xl[rows, :] = low
        transform(0, b)

    pl.semaphore_wait(barrier, DEVICES - 1)
    own(0).start()
    for disp in order:
        remote(0, disp).start()

    @pl.loop(0, 4)
    def _(b):
        transform(1, b)

    own(1).start()
    for disp in order:
        remote(1, disp).start()

    prim_copy.wait()

    wide = lax.broadcasted_iota(jnp.int32, (32, 128), 1)
    odd, upper = (wide // 32) % 2 == 1, wide >= 64
    lanes = lax.broadcasted_iota(jnp.int32, (1, 128), 1)
    total = jnp.zeros((1, 128), F32)

    def put(high_ref, low_ref, index, value):
        high, low = halves(value)
        high_ref[index] = high
        low_ref[index] = low

    def pair(high_ref, low_ref, index):
        return high_ref[index], low_ref[index]

    for j in range(2):
        put(ah, al, 0, prim[j, 0] + prim[j, 1])
        put(ah, al, 1, prim[j, 0])
        put(ah, al, 2, prim[j, 1])

        arrived = pltpu.make_async_remote_copy(
            src_ref=sbuf.at[pl.ds(j * DEVICES * 32, 127 * 32)],
            dst_ref=rbuf.at[pl.ds(j * DEVICES * 32, 127 * 32)],
            send_sem=send_sem.at[j],
            recv_sem=recv_sem.at[j],
            device_id=target(order[0]),
            device_id_type=MESH,
        )
        own(j).wait()
        arrived.wait_recv()

        @pl.loop(0, 8)
        def _(s):
            for x in range(4):
                v = [rbuf[piece(j, s * 16 + x * 4 + q), :] for q in range(4)]
                for m in (0, 2):
                    a, b = v[m], v[m + 1]
                    v[m] = jnp.where(odd, pltpu.roll(b, 32, 1), a)
                    v[m + 1] = jnp.where(odd, b, pltpu.roll(a, 96, 1))
                for m in (0, 1):
                    a, b = v[m], v[m + 2]
                    v[m] = jnp.where(upper, pltpu.roll(b, 64, 1), a)
                    v[m + 2] = jnp.where(upper, b, pltpu.roll(a, 64, 1))
                for g in range(4):
                    rows = pl.ds(pl.multiple_of(s * 64 + g * 16, 16), 16)
                    whole[0, rows, x * 128 : x * 128 + 128] = v[g][:16]
                    whole[1, rows, x * 128 : x * 128 + 128] = v[g][16:]

        for p in range(4):
            for q in range(p, 4):
                a, b = slice(p * 128, p * 128 + 128), slice(q * 128, q * 128 + 128)
                parts = []
                for c in range(2):
                    value = 0.5 * (whole[c, a, b] + whole[c, b, a].T)
                    whole[c, a, b] = value
                    parts.append((value, value.T if p != q else None))
                for where_, (re, im) in (((a, b), (parts[0][0], parts[1][0])), ((b, a), (parts[0][1], parts[1][1]))):
                    if re is None:
                        continue
                    if where_ == (b, a) and p != q:
                        whole[0, b, a] = re
                        whole[1, b, a] = im
                    for index, value in enumerate((re, im - re, re + im, im)):
                        high, low = halves(value)
                        dh[index, where_[0], where_[1]] = high
                        dl[index, where_[0], where_[1]] = low

        d_re, d_dif, d_sum, d_im = (pair(dh, dl, i) for i in range(4))
        first = dot3(pair(ah, al, 0), d_re)
        second = dot3(pair(ah, al, 1), d_dif)
        third = dot3(pair(ah, al, 2), d_sum)
        re = whole[0] - (first - third)
        im = whole[1] - (first + second)
        resid[j, 0] = re
        resid[j, 1] = im
        put(rh, rl, 0, re + im)
        put(rh, rl, 1, re)
        put(rh, rl, 2, im)
        cross = -dot3(d_sum, d_dif)
        flipped = cross.T
        square = dot3(d_im, d_im)
        h_re = 0.5 * (cross + flipped) + 2.0 * square
        h_im = 0.5 * (flipped - cross)
        put(hh, hl, 0, h_re)
        put(hh, hl, 1, h_im - h_re)
        put(hh, hl, 2, h_im + h_re)
        first = dot3(pair(rh, rl, 0), pair(hh, hl, 0))
        second = dot3(pair(rh, rl, 1), pair(hh, hl, 1))
        third = dot3(pair(rh, rl, 2), pair(hh, hl, 2))
        re = first - third
        im = first + second
        pred[j, 0] = re
        pred[j, 1] = im
        numer = jnp.sum(resid[j, 0] * re + resid[j, 1] * im, axis=0, keepdims=True)
        denom = jnp.sum(re * re + im * im, axis=0, keepdims=True)
        fold = []
        for value in (numer, denom):
            value = value[:, :128] + value[:, 128:256] + value[:, 256:384] + value[:, 384:]
            fold.append(value + pltpu.roll(value, 64, 1))
        total += weight_ref[j : j + 1, :] * jnp.where(lanes < 64, fold[0], fold[1])
        pltpu.make_async_copy(resid.at[j], resid_out.at[j], out_sem.at[j, 0]).start()
        pltpu.make_async_copy(pred.at[j], pred_out.at[j], out_sem.at[j, 1]).start()
        arrived.wait_send()

    stat[0] = total
    slots[me] = total

    def share(disp):
        return pltpu.make_async_remote_copy(
            src_ref=stat.at[0],
            dst_ref=slots.at[me],
            send_sem=stat_send,
            recv_sem=stat_recv,
            device_id=target(disp),
            device_id_type=MESH,
        )

    for disp in order:
        share(disp).start()
    done = pltpu.make_async_remote_copy(
        src_ref=slots.at[pl.ds(0, 127)],
        dst_ref=slots.at[pl.ds(0, 127)],
        send_sem=stat_send,
        recv_sem=stat_recv,
        device_id=target(order[0]),
        device_id_type=MESH,
    )
    done.wait_recv()
    every = jnp.sum(slots[...], axis=0)
    numer = jnp.sum(jnp.where(lanes < 64, every, 0.0), axis=1, keepdims=True)
    denom = jnp.sum(jnp.where(lanes < 64, 0.0, every), axis=1, keepdims=True)
    step_out[...] = jnp.broadcast_to(numer / denom, (8, 128))
    done.wait_send()
    for j in range(2):
        pltpu.make_async_copy(resid.at[j], resid_out.at[j], out_sem.at[j, 0]).wait()
        pltpu.make_async_copy(pred.at[j], pred_out.at[j], out_sem.at[j, 1]).wait()


def on_device(traces, freq_index, primaries):
    me = lax.axis_index("src") * 16 + lax.axis_index("rcv")
    samples = traces.shape[2]
    freq = jnp.broadcast_to(freq_index.reshape(DEVICES, 2).T.reshape(256, 1), (256, 128))
    weight = lax.dynamic_slice_in_dim(freq_index, me * 2, 2).astype(F32) / (samples // 2)
    weight = jnp.broadcast_to(weight[:, None], (2, 128))
    anywhere, vmem = pl.BlockSpec(memory_space=pl.ANY), pl.BlockSpec(memory_space=pltpu.VMEM)
    big = jax.ShapeDtypeStruct((2, 2, N, N), F32)
    dma = pltpu.SemaphoreType.DMA
    resid, pred, step = pl.pallas_call(
        kernel,
        out_shape=(big, big, jax.ShapeDtypeStruct((8, 128), F32)),
        in_specs=[anywhere, vmem, vmem, anywhere],
        out_specs=(anywhere, anywhere, vmem),
        scratch_shapes=[
            pltpu.VMEM((4, 4, 4, 32, 1024), F32),
            pltpu.VMEM((2048, 1024), BF16),
            pltpu.VMEM((2048, 1024), BF16),
            pltpu.VMEM((2, 256, 1024), BF16),
            pltpu.VMEM((2, 256, 1024), BF16),
            pltpu.VMEM((2 * DEVICES * 32, 128), F32),
            pltpu.VMEM((2 * DEVICES * 32, 128), F32),
            pltpu.VMEM((2, 2, N, N), F32),
            pltpu.VMEM((3, N, N), BF16),
            pltpu.VMEM((3, N, N), BF16),
            pltpu.VMEM((2, N, N), F32),
            pltpu.VMEM((4, N, N), BF16),
            pltpu.VMEM((4, N, N), BF16),
            pltpu.VMEM((3, N, N), BF16),
            pltpu.VMEM((3, N, N), BF16),
            pltpu.VMEM((3, N, N), BF16),
            pltpu.VMEM((3, N, N), BF16),
            pltpu.VMEM((2, 2, N, N), F32),
            pltpu.VMEM((2, 2, N, N), F32),
            pltpu.VMEM((1, 1, 128), F32),
            pltpu.VMEM((DEVICES, 1, 128), F32),
            dma((4,)), dma, dma((2,)), dma((2,)), dma((2,)), dma((2, 2)), dma, dma,
        ],
        compiler_params=pltpu.CompilerParams(
            collective_id=0, has_side_effects=True, vmem_limit_bytes=64 * 2**20 - 65536
        ),
    )(traces.reshape(4, 16, 32, samples), freq, weight, primaries)
    return (resid, resid - step[0, 0] * pred)


def solution(mesh):
    spec = P(("src", "rcv"), None, None, None)
    return jax.shard_map(
        on_device, mesh=mesh, in_specs=(P("src", "rcv", None), P(), spec), out_specs=(spec, spec), check_vma=False
    )
```

time: 279 us -> 94.4 us (0.34); the launches traced: 274 us -> 94.2 us
  Pallas kernels: 0 us -> 79.8 us
  blocking collectives: 63.8 us -> 0 us
  matrix products: 63.4 us -> 0 us
  local copies, waits for them, and re-layouts: 63.5 us -> 5.49 us
  waiting for transfers between devices: 51.5 us -> 0 us
  starting transfers between devices: 12.7 us -> 0 us
  other arithmetic: 16.8 us -> 8.21 us
    pallas_call x0 -> x1, Pallas kernels: none -> 79.8 us  [on_device(): pl.pallas_call(kernel, out_shape=(big, big, jax.ShapeDtypeStruct((8, 128)...]
    psum x1 -> x0, blocking collectives: 63.8 us -> none  [on_device(): numer, denom = lax.psum((numer, denom), ('src', 'rcv'))]
    dot_general x13 -> x0, matrix products: 63.4 us -> none  [the longest x12 47 us: matrix_product(): jnp.einsum('fij,fjk->fik', left, right, precision=lax.Precision.HIGHEST)]
    all_to_all x1 -> x0, waiting for transfers between devices: 51.5 us -> none  [on_device(): lax.all_to_all(spectrum, ('src', 'rcv'), split_axis=1, concat_axis=0, til...]
    reshape x2 -> x1, local copies, waits for them, and re-layouts: 18.8 us -> 0.81 us  [on_device(): freq_index.reshape(DEVICES, 2).T.reshape(256, 1)]
    unnamed x12 -> x3, local copies, waits for them, and re-layouts: 15.3 us -> 2.02 us
    transpose x1, local copies, waits for them, and re-layouts: 12.8 us -> 0.06 us  [on_device(): freq_index.reshape(DEVICES, 2).T.reshape(256, 1)]
    all_to_all x1 -> x0, starting transfers between devices: 12.7 us -> none  [on_device(): lax.all_to_all(spectrum, ('src', 'rcv'), split_axis=1, concat_axis=0, til...]
  transfers between devices with their start and end apart: 1 -> 0, of which waited for: 1 -> 0; matrix products, arithmetic and copies ran while one was open for 0% -> 0% of each run, Pallas kernels for 0% -> 0%
where the time goes in v1:
time: 94.4 us; the launch traced here: 94.2 us
  Pallas kernels  79.8 us (85%)
  other arithmetic  8.21 us (9%)
  local copies, waits for them, and re-layouts  5.49 us (6%)
    pallas_call x1, Pallas kernels, on_device(): pl.pallas_call(kernel, out_shape=(big, big, jax.ShapeDtypeStruct((8, 128)...  79.8 us
    sub x1, other arithmetic, on_device(): return (resid, resid - step[0, 0] * pred)  7.45 us
    unnamed x3, local copies, waits for them, and re-layouts  2.02 us

profile of v1, /device:TPU:1, one launch (start us, length us, event | category | flops | bytes accessed | tf_op | source)
XLA Modules:
  0.0 94.2 jit_solution(7309010123358087740)
XLA Ops:
  0.6 0.8 convert_multiply_fusion
  1.4 0.6 broadcast_in_dim.15.weight_ref
  2.0 0.8 reshape.14
  2.8 0.1 copy.5
  2.9 0.8 broadcast_in_dim.14.freq_ref
  3.7 79.8 %shard_map.50 = (f32[2,2,512,512]{3,2,1,0:T(8,128)}, f32[2,2,512,512]{3,2,1,0:T(8,128)}, f32[8,128]{1,0:T(8,128)}) custom-call(f32[4,16,32,1024]{3,2,1,0:T(8,128)} %bitcast.4, s32[256,128]{1,0:T(8,128)} %broadcast_in_dim.14.freq_ref, f32[2,128]{1,0:T(2,128)} %broadcast_in_dim.15.weight_ref, f32[2,2,512,512]{3,2,1,0:T(8,128)} %prim_ref.1), custom_call_target="tpu_custom_call" | custom-call | tf_op jit(solution)/shard_map/pallas_call | solution.py:304
  83.5 1.2 %slice.3 = f32[1,1]{1,0:T(1,128)} slice(f32[8,128]{1,0:T(8,128)} %get-tuple-element.6), slice={[0:1], [0:1]} | slice | bytes 8 | tf_op jit(solution)/shard_map/slice | solution.py:337
  84.7 0.0 copy-start
  84.7 7.4 %multiply_subtract_fusion = f32[2,2,512,512]{3,2,1,0:T(8,128)} fusion(f32[2,2,512,512]{3,2,1,0:T(8,128)} %get-tuple-element.10, f32[2,2,512,512]{3,2,1,0:T(8,128)} %get-tuple-element.7, f32[]{:T(128)} %bitcast.3), kind=kLoop, calls=%fused_computation | loop fusion | flops 2097152 | bytes 12582916 | tf_op jit(solution)/shard_map/sub | solution.py:337
  92.2 0.0 copy-done
  92.2 2.0 %copy.7 = f32[2,2,512,512]{3,2,1,0:T(8,128)} copy(f32[2,2,512,512]{3,2,1,0:T(8,128)S(1)} %copy-done) | data formatting | bytes 8388608
Async XLA Ops:
  84.7 7.5 %copy-start = (f32[2,2,512,512]{3,2,1,0:T(8,128)S(1)}, f32[2,2,512,512]{3,2,1,0:T(8,128)}, u32[]{:S(2)}) copy-start(f32[2,2,512,512]{3,2,1,0:T(8,128)} %get-tuple-element.10) | copy-start | bytes 12582916

commit v2 on v1

v2 whole, which is shorter than its diff:
```python
import math
import random

import jax
import jax.numpy as jnp
from jax import lax
from jax.experimental import pallas as pl
from jax.experimental.pallas import tpu as pltpu
from jax.sharding import PartitionSpec as P

MESH = pl.DeviceIdType.MESH
F32, BF16 = jnp.float32, jnp.bfloat16
NN = (((1,), (0,)), ((), ()))
NT = (((1,), (1,)), ((), ()))
N = 512
DEVICES = 128


def relative_groups():
    every = [(x, y, z) for x in range(4) for y in range(4) for z in range(2)]
    random.Random(0).shuffle(every)
    return [every[i : i + 4] for i in range(0, 32, 4)]


def halves(x):
    high = x.astype(BF16)
    return high, (x - high.astype(F32)).astype(BF16)


def dot3(left, right, dims=NN):
    def one(a, b):
        return lax.dot_general(a, b, dims, preferred_element_type=F32)

    return one(left[0], right[0]) + (one(left[0], right[1]) + one(left[1], right[0]))


def cos_sin(steps):
    quarter = (steps + 128) >> 8
    angle = (steps - quarter * 256).astype(F32) * (2.0 * math.pi / 1024)
    square = angle * angle
    cos = 1.0 / 40320 - square * (1.0 / 3628800)
    for term in (-1.0 / 720, 1.0 / 24, -0.5, 1.0):
        cos = term + square * cos
    sin = -1.0 / 5040 + square * (1.0 / 362880)
    for term in (1.0 / 120, -1.0 / 6, 1.0):
        sin = term + square * sin
    sin = angle * sin
    quarter = quarter & 3
    odd = (quarter & 1) == 1
    cos, sin = jnp.where(odd, sin, cos), jnp.where(odd, cos, sin)
    cos = jnp.where((quarter == 1) | (quarter == 2), -cos, cos)
    sin = jnp.where(quarter >= 2, -sin, sin)
    return cos, sin


def kernel(
    freq_ref, traces_ref, prim_ref,
    resid_out, pred_out, step_out,
    raw, xh, xl, th, tl, sbuf, rbuf, whole, ah, al, resid, pred, freqs, stat, slots,
    raw_sem, prim_sem, send_sem, recv_sem, own_sem, out_sem, stat_send, stat_recv,
):
    src, rcv = lax.axis_index("src"), lax.axis_index("rcv")
    me = src * 16 + rcv
    xs = [(rcv // 4 + d) % 4 for d in range(4)]
    ys = [(src // 2 + d) % 4 for d in range(4)]
    z_low = [(src + d) % 2 for d in range(2)]
    z_high = [(rcv // 2 + d) % 2 for d in range(2)]
    cores = [(rcv + d) % 2 for d in range(2)]
    groups = relative_groups()

    def targets(group):
        x, y, z = group
        return [
            (ys[y] * 2 + z_low[z], xs[x] * 4 + z_high[h] * 2 + cores[c])
            for h in range(2)
            for c in range(2)
            if (x, y, z, h, c) != (0, 0, 0, 0, 0)
        ]

    everyone = [to for bunch in groups for group in bunch for to in targets(group)]
    home = [k for k, bunch in enumerate(groups) if (0, 0, 0) in bunch][0]

    def load(b, g):
        rows = pl.ds(b * 4, 4)
        return pltpu.make_async_copy(traces_ref.at[g, rows], raw.at[rows, g], raw_sem.at[b])

    for b in range(4):
        for g in range(4):
            load(b, g).start()

    barrier = pltpu.get_barrier_semaphore()
    for to in everyone:
        pl.semaphore_signal(barrier, inc=1, device_id=to, device_id_type=MESH)

    lane = lax.broadcasted_iota(jnp.int32, (128, 128), 1)

    def table(j):
        for d in range(128):
            freqs[d : d + 1, :] = jnp.full((1, 128), freq_ref[2 * d + j], jnp.int32)
        freq = freqs[...]
        cos, sin = cos_sin((freq * lane) & 1023)
        cos, sin = cos * 0.03125, sin * 0.03125
        turn_cos, turn_sin = cos_sin((freq * 128) & 1023)
        sign = 1.0 - 2.0 * (freq & 1).astype(F32)
        for a in range(4):
            if a:
                cos, sin = cos * turn_cos - sin * turn_sin, sin * turn_cos + cos * turn_sin
            for c, part in enumerate((cos, -sin)):
                for k, value in ((a, part), (a + 4, part * sign)):
                    high, low = halves(value)
                    th[j, c * 128 : c * 128 + 128, k * 128 : k * 128 + 128] = high
                    tl[j, c * 128 : c * 128 + 128, k * 128 : k * 128 + 128] = low

    def transform(j, h, b):
        rows = pl.ds(pl.multiple_of((h * 2 + b) * 512, 512), 512)
        out = dot3((th[j], tl[j]), (xh[rows, :], xl[rows, :]), NT)
        for c in range(2):
            for d in range(0, 128, 8):
                for i in range(4):
                    start = ((j * 2 + h) * DEVICES + d) * 16 + c * 8 + b * 4 + i
                    sbuf[pl.ds(start, 8, stride=16), :] = out[
                        c * 128 + d : c * 128 + d + 8, i * 128 : i * 128 + 128
                    ]

    def piece(j, h, index, count=1):
        return pl.ds(pl.multiple_of(((j * 2 + h) * DEVICES + index) * 16, 16), 16 * count)

    def own(j, h):
        return pltpu.make_async_copy(sbuf.at[piece(j, h, me)], rbuf.at[piece(j, h, me)], own_sem.at[j * 2 + h])

    def send(j, h):
        own(j, h).start()
        for k, bunch in enumerate(groups):
            for group in bunch:
                for to in targets(group):
                    pltpu.make_async_remote_copy(
                        src_ref=sbuf.at[piece(j, h, to[0] * 16 + to[1])],
                        dst_ref=rbuf.at[piece(j, h, me)],
                        send_sem=send_sem.at[j * 2 + h],
                        recv_sem=recv_sem.at[(j * 2 + h) * 8 + k],
                        device_id=to,
                        device_id_type=MESH,
                    ).start()

    def arrival(j, h, k, count):
        return pltpu.make_async_remote_copy(
            src_ref=sbuf.at[piece(j, h, 0, count)],
            dst_ref=rbuf.at[piece(j, h, 0, count)],
            send_sem=send_sem.at[j * 2 + h],
            recv_sem=recv_sem.at[(j * 2 + h) * 8 + k],
            device_id=everyone[0],
            device_id_type=MESH,
        )

    table(0)
    for h in range(2):
        for b in range(2):
            n = h * 2 + b
            for g in range(4):
                load(n, g).wait()
            high, low = halves(raw[n * 4 : n * 4 + 4].reshape(512, 1024))
            xh[n * 512 : n * 512 + 512, :] = high
            xl[n * 512 : n * 512 + 512, :] = low
            transform(0, h, b)
        if h == 0:
            pl.semaphore_wait(barrier, DEVICES - 1)
        send(0, h)

    def prim_copy(j, c):
        return pltpu.make_async_copy(
            prim_ref.at[j, c], raw.at[pl.ds(4 * c, 4), :, :, pl.ds(j * N, N)], prim_sem.at[j * 2 + c]
        )

    for j in range(2):
        for c in range(2):
            prim_copy(j, c).start()

    table(1)
    for h in range(2):
        for b in range(2):
            transform(1, h, b)
        send(1, h)

    wide = lax.broadcasted_iota(jnp.int32, (16, 128), 1)
    odd, upper = (wide // 32) % 2 == 1, wide >= 64
    lanes = lax.broadcasted_iota(jnp.int32, (1, 128), 1)
    total = jnp.zeros((1, 128), F32)

    def put(slot, value):
        high, low = halves(value)
        rows, columns = slice(slot % 4 * N, slot % 4 * N + N), slice(slot // 4 * N, slot // 4 * N + N)
        xh[rows, columns] = high
        xl[rows, columns] = low

    def get(slot):
        rows, columns = slice(slot % 4 * N, slot % 4 * N + N), slice(slot // 4 * N, slot // 4 * N + N)
        return xh[rows, columns], xl[rows, columns]

    for j in range(2):
        for c in range(2):
            prim_copy(j, c).wait()
        model = [raw[4 * c : 4 * c + 4, :, :, j * N : j * N + N].reshape(N, N) for c in range(2)]
        for index, value in enumerate((model[0] + model[1], model[0], model[1])):
            high, low = halves(value)
            ah[index] = high
            al[index] = low

        @pl.loop(0, 2)
        def _(h):
            for k, bunch in enumerate(groups):
                if k == home:
                    own(j, h).wait()
                arrival(j, h, k, 15 if k == home else 16).wait_recv()
                for x, y, z in bunch:
                    from_x, from_s = xs[-x % 4], ys[-y % 4] * 2 + z_low[z]
                    v = [rbuf[piece(j, h, from_s * 16 + from_x * 4 + q), :] for q in range(4)]
                    for m in (0, 2):
                        a, b = v[m], v[m + 1]
                        v[m] = jnp.where(odd, pltpu.roll(b, 32, 1), a)
                        v[m + 1] = jnp.where(odd, b, pltpu.roll(a, 96, 1))
                    for m in (0, 1):
                        a, b = v[m], v[m + 2]
                        v[m] = jnp.where(upper, pltpu.roll(b, 64, 1), a)
                        v[m + 2] = jnp.where(upper, b, pltpu.roll(a, 64, 1))
                    columns = pl.ds(pl.multiple_of(from_x * 128, 128), 128)
                    for g in range(4):
                        rows = pl.ds(pl.multiple_of(from_s * 64 + g * 16 + h * 8, 8), 8)
                        whole[0, rows, columns] = v[g][:8]
                        whole[1, rows, columns] = v[g][8:]

        for p in range(4):
            for q in range(p, 4):
                a, b = slice(p * 128, p * 128 + 128), slice(q * 128, q * 128 + 128)
                parts = []
                for c in range(2):
                    value = 0.5 * (whole[c, a, b] + whole[c, b, a].T)
                    whole[c, a, b] = value
                    parts.append((value, value.T if p != q else None))
                for (rows, columns), t in (((a, b), 0), ((b, a), 1))[: 1 + (p != q)]:
                    re, im = parts[0][t], parts[1][t]
                    if t:
                        whole[0, rows, columns] = re
                        whole[1, rows, columns] = im
                    for index, value in enumerate((re, im - re, re + im, im)):
                        high, low = halves(value)
                        at = slice(index * N + rows.start, index * N + rows.stop)
                        xh[at, columns] = high
                        xl[at, columns] = low

        first = dot3((ah[0], al[0]), get(0))
        second = dot3((ah[1], al[1]), get(1))
        third = dot3((ah[2], al[2]), get(2))
        if j:
            for copy in out_copies(resid_out, pred_out, resid, pred, out_sem, 0):
                copy.wait()
        re = whole[0] - (first - third)
        im = whole[1] - (first + second)
        resid[0] = re
        resid[1] = im
        put(4, re + im)
        put(5, re)
        put(6, im)
        cross = -dot3(get(2), get(1))
        square = dot3(get(3), get(3))
        flipped = cross.T
        h_re = 0.5 * (cross + flipped) + 2.0 * square
        h_im = 0.5 * (flipped - cross)
        put(7, h_re)
        put(0, h_im - h_re)
        put(1, h_im + h_re)
        first = dot3(get(4), get(7))
        second = dot3(get(5), get(0))
        third = dot3(get(6), get(1))
        re = first - third
        im = first + second
        pred[0] = re
        pred[1] = im
        numer = jnp.sum(resid[0] * re + resid[1] * im, axis=0, keepdims=True)
        denom = jnp.sum(re * re + im * im, axis=0, keepdims=True)
        fold = []
        for value in (numer, denom):
            value = value[:, :128] + value[:, 128:256] + value[:, 256:384] + value[:, 384:]
            fold.append(value + pltpu.roll(value, 64, 1))
        weight = freq_ref[me * 2 + j].astype(F32) * (1.0 / 512)
        total += weight * jnp.where(lanes < 64, fold[0], fold[1])
        for copy in out_copies(resid_out, pred_out, resid, pred, out_sem, j):
            copy.start()

    stat[0] = total
    slots[me] = total
    for to in everyone:
        pltpu.make_async_remote_copy(
            src_ref=stat.at[0],
            dst_ref=slots.at[me],
            send_sem=stat_send,
            recv_sem=stat_recv,
            device_id=to,
            device_id_type=MESH,
        ).start()
    done = pltpu.make_async_remote_copy(
        src_ref=slots.at[pl.ds(0, 127)],
        dst_ref=slots.at[pl.ds(0, 127)],
        send_sem=stat_send,
        recv_sem=stat_recv,
        device_id=everyone[0],
        device_id_type=MESH,
    )
    for j in range(2):
        for h in range(2):
            arrival(j, h, 0, 127).wait_send()
    done.wait_recv()
    every = jnp.sum(slots[...], axis=0)
    numer = jnp.sum(jnp.where(lanes < 64, every, 0.0), axis=1, keepdims=True)
    denom = jnp.sum(jnp.where(lanes < 64, 0.0, every), axis=1, keepdims=True)
    step_out[...] = jnp.broadcast_to(numer / denom, (8, N))
    done.wait_send()
    for copy in out_copies(resid_out, pred_out, resid, pred, out_sem, 1):
        copy.wait()


def out_copies(resid_out, pred_out, resid, pred, sem, j):
    return (
        pltpu.make_async_copy(resid, resid_out.at[j], sem.at[j, 0]),
        pltpu.make_async_copy(pred, pred_out.at[j], sem.at[j, 1]),
    )


def on_device(traces, freq_index, primaries):
    samples = traces.shape[2]
    anywhere, vmem = pl.BlockSpec(memory_space=pl.ANY), pl.BlockSpec(memory_space=pltpu.VMEM)
    big = jax.ShapeDtypeStruct((2, 2, N, N), F32)
    dma = pltpu.SemaphoreType.DMA
    resid, pred, step = pl.pallas_call(
        kernel,
        out_shape=(big, big, jax.ShapeDtypeStruct((8, N), F32)),
        in_specs=[pl.BlockSpec(memory_space=pltpu.SMEM), anywhere, anywhere],
        out_specs=(anywhere, anywhere, vmem),
        scratch_shapes=[
            pltpu.VMEM((16, 4, 32, 1024), F32),
            pltpu.VMEM((2048, 1024), BF16),
            pltpu.VMEM((2048, 1024), BF16),
            pltpu.VMEM((2, 256, 1024), BF16),
            pltpu.VMEM((2, 256, 1024), BF16),
            pltpu.VMEM((4 * DEVICES * 16, 128), F32),
            pltpu.VMEM((4 * DEVICES * 16, 128), F32),
            pltpu.VMEM((2, N, N), F32),
            pltpu.VMEM((3, N, N), BF16),
            pltpu.VMEM((3, N, N), BF16),
            pltpu.VMEM((2, N, N), F32),
            pltpu.VMEM((2, N, N), F32),
            pltpu.VMEM((128, 128), jnp.int32),
            pltpu.VMEM((1, 1, 128), F32),
            pltpu.VMEM((DEVICES, 1, 128), F32),
            dma((4,)), dma((4,)), dma((4,)), dma((32,)), dma((4,)), dma((2, 2)), dma, dma,
        ],
        compiler_params=pltpu.CompilerParams(
            collective_id=0, has_side_effects=True, vmem_limit_bytes=44 * 2**20
        ),
    )(freq_index, traces.reshape(4, 16, 32, samples), primaries.reshape(2, 2, 4, 4, 32, N))
    tiles = (2, 2, N // 8, 8, N)
    update = resid.reshape(tiles) - step * pred.reshape(tiles)
    return (resid, update.reshape(resid.shape))


def solution(mesh):
    spec = P(("src", "rcv"), None, None, None)
    return jax.shard_map(
        on_device, mesh=mesh, in_specs=(P("src", "rcv", None), P(), spec), out_specs=(spec, spec), check_vma=False
    )
```

time: 94.4 us -> 83.6 us (0.89)
  other arithmetic: 8.21 us -> 3.18 us
  Pallas kernels: 79.8 us -> 76.8 us
  local copies, waits for them, and re-layouts: 5.49 us -> 2.8 us
    sub x1, other arithmetic: 7.45 us -> 3.18 us  [on_device(): update = resid.reshape(tiles) - step * pred.reshape(tiles)]
    pallas_call x1, Pallas kernels: 79.8 us -> 76.8 us  [on_device(): pl.pallas_call(kernel, out_shape=(big, big, jax.ShapeDtypeStruct((8, N),...]
    broadcast_in_dim x2 -> x0, local copies, waits for them, and re-layouts: 1.41 us -> none  [the longest x1 0.78 us: on_device(): jnp.broadcast_to(freq_index.reshape(DEVICES, 2).T.reshape(256, 1), (256,...]
    slice x1 -> x0, local copies, waits for them, and re-layouts: 1.19 us -> none  [on_device(): return (resid, resid - step[0, 0] * pred)]
where the time goes in v2:
time: 83.6 us; the launch traced here: 83.4 us
  Pallas kernels  76.8 us (92%)
  other arithmetic  3.18 us (4%)
  local copies, waits for them, and re-layouts  2.8 us (3%)
    pallas_call x1, Pallas kernels, on_device(): pl.pallas_call(kernel, out_shape=(big, big, jax.ShapeDtypeStruct((8, N),...  76.8 us
    sub x1, other arithmetic, on_device(): update = resid.reshape(tiles) - step * pred.reshape(tiles)  3.18 us
    unnamed x3, local copies, waits for them, and re-layouts  2.68 us

profile of v2, /device:TPU:1, one launch (start us, length us, event | category | flops | bytes accessed | tf_op | source)
XLA Modules:
  0.0 83.4 jit_solution(8309208463474246892)
XLA Ops:
  0.6 0.0 copy-start
  0.6 0.7 copy-done
  1.3 76.8 %shard_map.50 = (f32[2,2,512,512]{3,2,1,0:T(8,128)S(1)}, f32[2,2,512,512]{3,2,1,0:T(8,128)S(1)}, f32[8,512]{1,0:T(8,128)S(1)}) custom-call(s32[256]{0:T(256)S(1)} %copy-done, f32[4,16,32,1024]{3,2,1,0:T(8,128)} %bitcast.4, f32[2,2,4,4,32,512]{5,4,3,2,1,0:T(8,128)} %bitcast.5), custom_call_target="tpu_custom_call" | custom-call | tf_op jit(solution)/shard_map/pallas_call | solution.py:333
  78.1 0.1 broadcast_bitcast_fusion
  78.2 3.2 %multiply_subtract_fusion = f32[2,2,512,512]{3,2,1,0:T(8,128)} fusion(f32[2,2,512,512]{3,2,1,0:T(8,128)S(1)} %get-tuple-element.10, f32[2,2,512,512]{3,2,1,0:T(8,128)S(1)} %get-tuple-element.7, f32[512,512]{1,0:T(8,128)S(1)} %broadcast_bitcast_fusion), kind=kLoop, calls=%fused_computation | loop fusion | flops 2097152 | bytes 13631488 | tf_op jit(solution)/shard_map/sub | solution.py:361
  81.4 2.0 %copy.6 = f32[2,2,512,512]{3,2,1,0:T(8,128)} copy(f32[2,2,512,512]{3,2,1,0:T(8,128)S(1)} %get-tuple-element.10) | data formatting | bytes 8388608
Async XLA Ops:
  0.6 0.7 copy-start

commit v3 on v2

--- a/solution.py
+++ b/solution.py
@@ -14,6 +14,10 @@
 NT = (((1,), (1,)), ((), ()))
 N = 512
 DEVICES = 128
+
+
+def far(x, y, z=0, h=0, c=0):
+    return min(x, 4 - x) + min(y, 4 - y) + (0, 2, 1, 1)[2 * z + h]
 
 
 def relative_groups():
@@ -54,10 +58,10 @@
 
 
 def kernel(
-    freq_ref, traces_ref, prim_ref,
+    freq_hbm, traces_ref, prim_ref,
     resid_out, pred_out, step_out,
-    raw, xh, xl, th, tl, sbuf, rbuf, whole, ah, al, resid, pred, freqs, stat, slots,
-    raw_sem, prim_sem, send_sem, recv_sem, own_sem, out_sem, stat_send, stat_recv,
+    raw, xh, xl, th, tl, sbuf, rbuf, whole, ah, al, resid, pred, freq_ref, freqs, stat, slots,
+    freq_sem, raw_sem, prim_sem, send_sem, recv_sem, own_sem, out_sem, stat_send, stat_recv,
 ):
     src, rcv = lax.axis_index("src"), lax.axis_index("rcv")
     me = src * 16 + rcv
@@ -77,13 +81,17 @@
             if (x, y, z, h, c) != (0, 0, 0, 0, 0)
         ]
 
-    everyone = [to for bunch in groups for group in bunch for to in targets(group)]
+    offsets = [(x, y, z, h, c) for x in range(4) for y in range(4) for z in range(2) for h in range(2) for c in range(2)]
+    offsets = sorted(offsets[1:], key=lambda offset: -far(*offset))
+    everyone = [(ys[y] * 2 + z_low[z], xs[x] * 4 + z_high[h] * 2 + cores[c]) for x, y, z, h, c in offsets]
     home = [k for k, bunch in enumerate(groups) if (0, 0, 0) in bunch][0]
 
     def load(b, g):
         rows = pl.ds(b * 4, 4)
         return pltpu.make_async_copy(traces_ref.at[g, rows], raw.at[rows, g], raw_sem.at[b])
 
+    freq_copy = pltpu.make_async_copy(freq_hbm, freq_ref, freq_sem)
+    freq_copy.start()
     for b in range(4):
         for g in range(4):
             load(b, g).start()
@@ -111,16 +119,27 @@
                     th[j, c * 128 : c * 128 + 128, k * 128 : k * 128 + 128] = high
                     tl[j, c * 128 : c * 128 + 128, k * 128 : k * 128 + 128] = low
 
-    def transform(j, h, b):
-        rows = pl.ds(pl.multiple_of((h * 2 + b) * 512, 512), 512)
-        out = dot3((th[j], tl[j]), (xh[rows, :], xl[rows, :]), NT)
+    def transform(h, b):
+        rows = slice((h * 2 + b) * 512, (h * 2 + b) * 512 + 512)
+        out = dot3((th[0], tl[0]), (xh[rows, :], xl[rows, :]), NT)
         for c in range(2):
             for d in range(0, 128, 8):
                 for i in range(4):
-                    start = ((j * 2 + h) * DEVICES + d) * 16 + c * 8 + b * 4 + i
+                    start = (h * DEVICES + d) * 16 + c * 8 + b * 4 + i
                     sbuf[pl.ds(start, 8, stride=16), :] = out[
                         c * 128 + d : c * 128 + d + 8, i * 128 : i * 128 + 128
                     ]
+
+    def transform_part(c):
+        @pl.loop(0, 4)
+        def _(b):
+            rows = pl.ds(pl.multiple_of(b * 512, 512), 512)
+            part = slice(c * 128, c * 128 + 128)
+            out = dot3((th[1, part], tl[1, part]), (xh[rows, :], xl[rows, :]), NT)
+            for d in range(0, 128, 8):
+                for i in range(4):
+                    start = ((2 + c) * DEVICES + d) * 16 + b * 4 + i
+                    sbuf[pl.ds(start, 8, stride=16), :] = out[d : d + 8, i * 128 : i * 128 + 128]
 
     def piece(j, h, index, count=1):
         return pl.ds(pl.multiple_of(((j * 2 + h) * DEVICES + index) * 16, 16), 16 * count)
@@ -152,6 +171,7 @@
             device_id_type=MESH,
         )
 
+    freq_copy.wait()
     table(0)
     for h in range(2):
         for b in range(2):
@@ -161,7 +181,7 @@
             high, low = halves(raw[n * 4 : n * 4 + 4].reshape(512, 1024))
             xh[n * 512 : n * 512 + 512, :] = high
             xl[n * 512 : n * 512 + 512, :] = low
-            transform(0, h, b)
+            transform(h, b)
         if h == 0:
             pl.semaphore_wait(barrier, DEVICES - 1)
         send(0, h)
@@ -176,10 +196,9 @@
             prim_copy(j, c).start()
 
     table(1)
-    for h in range(2):
-        for b in range(2):
-            transform(1, h, b)
-        send(1, h)
+    for c in range(2):
+        transform_part(c)
+        send(1, c)
 
     wide = lax.broadcasted_iota(jnp.int32, (16, 128), 1)
     odd, upper = (wide // 32) % 2 == 1, wide >= 64
@@ -196,7 +215,7 @@
         rows, columns = slice(slot % 4 * N, slot % 4 * N + N), slice(slot // 4 * N, slot // 4 * N + N)
         return xh[rows, columns], xl[rows, columns]
 
-    for j in range(2):
+    def model_operands(j):
         for c in range(2):
             prim_copy(j, c).wait()
         model = [raw[4 * c : 4 * c + 4, :, :, j * N : j * N + N].reshape(N, N) for c in range(2)]
@@ -205,72 +224,100 @@
             ah[index] = high
             al[index] = low
 
-        @pl.loop(0, 2)
-        def _(h):
-            for k, bunch in enumerate(groups):
-                if k == home:
-                    own(j, h).wait()
-                arrival(j, h, k, 15 if k == home else 16).wait_recv()
-                for x, y, z in bunch:
-                    from_x, from_s = xs[-x % 4], ys[-y % 4] * 2 + z_low[z]
-                    v = [rbuf[piece(j, h, from_s * 16 + from_x * 4 + q), :] for q in range(4)]
-                    for m in (0, 2):
-                        a, b = v[m], v[m + 1]
-                        v[m] = jnp.where(odd, pltpu.roll(b, 32, 1), a)
-                        v[m + 1] = jnp.where(odd, b, pltpu.roll(a, 96, 1))
-                    for m in (0, 1):
-                        a, b = v[m], v[m + 2]
-                        v[m] = jnp.where(upper, pltpu.roll(b, 64, 1), a)
-                        v[m + 2] = jnp.where(upper, b, pltpu.roll(a, 64, 1))
-                    columns = pl.ds(pl.multiple_of(from_x * 128, 128), 128)
-                    for g in range(4):
-                        rows = pl.ds(pl.multiple_of(from_s * 64 + g * 16 + h * 8, 8), 8)
-                        whole[0, rows, columns] = v[g][:8]
-                        whole[1, rows, columns] = v[g][8:]
-
+    def assemble(j, h, store):
+        for k, bunch in enumerate(groups):
+            if k == home:
+                own(j, h).wait()
+            arrival(j, h, k, 15 if k == home else 16).wait_recv()
+            for x, y, z in bunch:
+                from_x, from_s = xs[-x % 4], ys[-y % 4] * 2 + z_low[z]
+                v = [rbuf[piece(j, h, from_s * 16 + from_x * 4 + q), :] for q in range(4)]
+                for m in (0, 2):
+                    a, b = v[m], v[m + 1]
+                    v[m] = jnp.where(odd, pltpu.roll(b, 32, 1), a)
+                    v[m + 1] = jnp.where(odd, b, pltpu.roll(a, 96, 1))
+                for m in (0, 1):
+                    a, b = v[m], v[m + 2]
+                    v[m] = jnp.where(upper, pltpu.roll(b, 64, 1), a)
+                    v[m + 2] = jnp.where(upper, b, pltpu.roll(a, 64, 1))
+                columns = pl.ds(pl.multiple_of(from_x * 128, 128), 128)
+                for g in range(4):
+                    store(h, from_s * 64 + g * 16, columns, v[g])
+
+    def store_both(h, row, columns, value):
+        rows = pl.ds(pl.multiple_of(row + h * 8, 8), 8)
+        whole[0, rows, columns] = value[:8]
+        whole[1, rows, columns] = value[8:]
+
+    def store_part(c, row, columns, value):
+        whole[c, pl.ds(pl.multiple_of(row, 16), 16), columns] = value
+
+    def symmetric(c, then):
         for p in range(4):
             for q in range(p, 4):
                 a, b = slice(p * 128, p * 128 + 128), slice(q * 128, q * 128 + 128)
-                parts = []
-                for c in range(2):
-                    value = 0.5 * (whole[c, a, b] + whole[c, b, a].T)
-                    whole[c, a, b] = value
-                    parts.append((value, value.T if p != q else None))
-                for (rows, columns), t in (((a, b), 0), ((b, a), 1))[: 1 + (p != q)]:
-                    re, im = parts[0][t], parts[1][t]
-                    if t:
-                        whole[0, rows, columns] = re
-                        whole[1, rows, columns] = im
-                    for index, value in enumerate((re, im - re, re + im, im)):
-                        high, low = halves(value)
-                        at = slice(index * N + rows.start, index * N + rows.stop)
-                        xh[at, columns] = high
-                        xl[at, columns] = low
-
-        first = dot3((ah[0], al[0]), get(0))
-        second = dot3((ah[1], al[1]), get(1))
-        third = dot3((ah[2], al[2]), get(2))
-        if j:
+                value = 0.5 * (whole[c, a, b] + whole[c, b, a].T)
+                whole[c, a, b] = value
+                then(a, b, value)
+                if p != q:
+                    value = value.T
+                    whole[c, b, a] = value
+                    then(b, a, value)
+
+    def put_block(slot, rows, columns, value):
+        high, low = halves(value)
+        at = slice(slot * N + rows.start, slot * N + rows.stop)
+        xh[at, columns] = high
+        xl[at, columns] = low
+
+    def real_operands(rows, columns, value):
+        put_block(0, rows, columns, value)
+
+    def imag_operands(rows, columns, value):
+        real = whole[0, rows, columns]
+        put_block(1, rows, columns, value - real)
+        put_block(2, rows, columns, real + value)
+        put_block(3, rows, columns, value)
+
+    for j in range(2):
+        model_operands(j)
+        if j == 0:
+
+            @pl.loop(0, 2)
+            def _(h):
+                assemble(0, h, store_both)
+
+            symmetric(0, real_operands)
+            pred[0] = dot3((ah[0], al[0]), get(0))
+        else:
+            assemble(1, 0, store_part)
+            symmetric(0, real_operands)
             for copy in out_copies(resid_out, pred_out, resid, pred, out_sem, 0):
                 copy.wait()
-        re = whole[0] - (first - third)
-        im = whole[1] - (first + second)
-        resid[0] = re
-        resid[1] = im
-        put(4, re + im)
-        put(5, re)
-        put(6, im)
+            pred[0] = dot3((ah[0], al[0]), get(0))
+            assemble(1, 1, store_part)
+        symmetric(1, imag_operands)
+
         cross = -dot3(get(2), get(1))
         square = dot3(get(3), get(3))
+        second = dot3((ah[1], al[1]), get(1))
         flipped = cross.T
         h_re = 0.5 * (cross + flipped) + 2.0 * square
         h_im = 0.5 * (flipped - cross)
-        put(7, h_re)
-        put(0, h_im - h_re)
-        put(1, h_im + h_re)
-        first = dot3(get(4), get(7))
-        second = dot3(get(5), get(0))
-        third = dot3(get(6), get(1))
+        ah[0], al[0] = halves(h_re)
+        put(7, h_im - h_re)
+        put(0, h_im + h_re)
+        im = whole[1] - (pred[0] + second)
+        resid[1] = im
+        put(6, im)
+        third = dot3((ah[2], al[2]), get(2))
+        re = whole[0] - (pred[0] - third)
+        resid[0] = re
+        put(5, re)
+        put(4, re + im)
+        third = dot3(get(6), get(0))
+        second = dot3(get(5), get(7))
+        first = dot3(get(4), (ah[0], al[0]))
         re = first - third
         im = first + second
         pred[0] = re
@@ -283,8 +330,9 @@
             fold.append(value + pltpu.roll(value, 64, 1))
         weight = freq_ref[me * 2 + j].astype(F32) * (1.0 / 512)
         total += weight * jnp.where(lanes < 64, fold[0], fold[1])
-        for copy in out_copies(resid_out, pred_out, resid, pred, out_sem, j):
-            copy.start()
+        if j == 0:
+            for copy in out_copies(resid_out, pred_out, resid, pred, out_sem, 0):
+                copy.start()
 
     stat[0] = total
     slots[me] = total
@@ -297,6 +345,8 @@
             device_id=to,
             device_id_type=MESH,
         ).start()
+    for copy in out_copies(resid_out, pred_out, resid, pred, out_sem, 1):
+        copy.start()
     done = pltpu.make_async_remote_copy(
         src_ref=slots.at[pl.ds(0, 127)],
         dst_ref=slots.at[pl.ds(0, 127)],
@@ -325,6 +375,23 @@
     )
 
 
+def final_kernel(resid, pred, step, resid_out, next_out, new, resid_sem, next_sem):
+    copies = []
+    for j in range(2):
+        for c in range(2):
+            copies.append(pltpu.make_async_copy(resid.at[j, c], resid_out.at[j, c], resid_sem.at[j * 2 + c]))
+            copies[-1].start()
+            for half in range(2):
+                rows = slice(half * 256, half * 256 + 256)
+                value = resid[j, c, rows, :] - jnp.tile(step[...], (32, 1)) * pred[j, c, rows, :]
+                new[j, c, rows, :] = value
+                at = (j, c, pl.ds(half * 256, 256))
+                copies.append(pltpu.make_async_copy(new.at[at], next_out.at[at], next_sem.at[j * 4 + c * 2 + half]))
+                copies[-1].start()
+    for copy in copies:
+        copy.wait()
+
+
 def on_device(traces, freq_index, primaries):
     samples = traces.shape[2]
     anywhere, vmem = pl.BlockSpec(memory_space=pl.ANY), pl.BlockSpec(memory_space=pltpu.VMEM)
@@ -333,7 +400,7 @@
     resid, pred, step = pl.pallas_call(
         kernel,
         out_shape=(big, big, jax.ShapeDtypeStruct((8, N), F32)),
-        in_specs=[pl.BlockSpec(memory_space=pltpu.SMEM), anywhere, anywhere],
+        in_specs=[pl.BlockSpec(memory_space=pltpu.HBM), anywhere, anywhere],
         out_specs=(anywhere, anywhere, vmem),
         scratch_shapes=[
             pltpu.VMEM((16, 4, 32, 1024), F32),
@@ -348,18 +415,24 @@
             pltpu.VMEM((3, N, N), BF16),
             pltpu.VMEM((2, N, N), F32),
             pltpu.VMEM((2, N, N), F32),
+            pltpu.SMEM((256,), jnp.int32),
             pltpu.VMEM((128, 128), jnp.int32),
             pltpu.VMEM((1, 1, 128), F32),
             pltpu.VMEM((DEVICES, 1, 128), F32),
-            dma((4,)), dma((4,)), dma((4,)), dma((32,)), dma((4,)), dma((2, 2)), dma, dma,
+            dma, dma((4,)), dma((4,)), dma((4,)), dma((32,)), dma((4,)), dma((2, 2)), dma, dma,
         ],
         compiler_params=pltpu.CompilerParams(
             collective_id=0, has_side_effects=True, vmem_limit_bytes=44 * 2**20
         ),
     )(freq_index, traces.reshape(4, 16, 32, samples), primaries.reshape(2, 2, 4, 4, 32, N))
-    tiles = (2, 2, N // 8, 8, N)
-    update = resid.reshape(tiles) - step * pred.reshape(tiles)
-    return (resid, update.reshape(resid.shape))
+    return pl.pallas_call(
+        final_kernel,
+        out_shape=(big, big),
+        in_specs=[vmem, vmem, vmem],
+        out_specs=(anywhere, anywhere),
+        scratch_shapes=[pltpu.VMEM((2, 2, N, N), F32), dma((4,)), dma((8,))],
+        compiler_params=pltpu.CompilerParams(vmem_limit_bytes=16 * 2**20),
+    )(resid, pred, step)
 
 
 def solution(mesh):

time: 83.6 us -> 78.7 us (0.941)
  other arithmetic: 3.18 us -> 0 us
  local copies, waits for them, and re-layouts: 2.8 us -> 0.67 us
    pallas_call x0 -> x1, Pallas kernels: none -> 3.4 us  [on_device(): pl.pallas_call(final_kernel, out_shape=(big, big), in_specs=[vmem, vmem,...]
    sub x1 -> x0, other arithmetic: 3.18 us -> none  [on_device(): update = resid.reshape(tiles) - step * pred.reshape(tiles)]
    pallas_call x1, Pallas kernels: 76.8 us -> 73.6 us  [on_device(): pl.pallas_call(kernel, out_shape=(big, big, jax.ShapeDtypeStruct((8, N),...]
    unnamed x3 -> x2, local copies, waits for them, and re-layouts: 2.68 us -> 0.67 us
where the time goes in v3:
time: 78.7 us; the launch traced here: 78.5 us
  Pallas kernels  77 us (98%)
  between operations  0.83 us (1%)
    pallas_call x1, Pallas kernels, on_device(): pl.pallas_call(kernel, out_shape=(big, big, jax.ShapeDtypeStruct((8, N),...  73.6 us
    pallas_call x1, Pallas kernels, on_device(): pl.pallas_call(final_kernel, out_shape=(big, big), in_specs=[vmem, vmem,...  3.4 us

profile of v3, /device:TPU:1, one launch (start us, length us, event | category | flops | bytes accessed | tf_op | source)
XLA Modules:
  0.0 78.5 jit_solution(6709187865424351170)
XLA Ops:
  0.6 0.0 copy-start
  0.6 0.7 copy-done
  1.3 73.6 %shard_map.50 = (f32[2,2,512,512]{3,2,1,0:T(8,128)S(1)}, f32[2,2,512,512]{3,2,1,0:T(8,128)S(1)}, f32[8,512]{1,0:T(8,128)S(1)}) custom-call(s32[256]{0:T(256)S(1)} %copy-done, f32[4,16,32,1024]{3,2,1,0:T(8,128)} %bitcast.2, f32[2,2,4,4,32,512]{5,4,3,2,1,0:T(8,128)} %bitcast.3), custom_call_target="tpu_custom_call" | custom-call | tf_op jit(solution)/shard_map/pallas_call | solution.py:400
  75.0 3.4 %shard_map.51 = (f32[2,2,512,512]{3,2,1,0:T(8,128)}, f32[2,2,512,512]{3,2,1,0:T(8,128)}) custom-call(f32[2,2,512,512]{3,2,1,0:T(8,128)S(1)} %get-tuple-element.5.resid, f32[2,2,512,512]{3,2,1,0:T(8,128)S(1)} %get-tuple-element.6.pred, f32[8,512]{1,0:T(8,128)S(1)} %get-tuple-element.7.step), custom_call_target="tpu_custom_call" | custom-call | tf_op jit(solution)/shard_map/pallas_call | solution.py:428
Async XLA Ops:
  0.6 0.7 copy-start

commit v4 on v3

--- a/solution.py
+++ b/solution.py
@@ -20,10 +20,21 @@
     return min(x, 4 - x) + min(y, 4 - y) + (0, 2, 1, 1)[2 * z + h]
 
 
+def far_first():
+    every = [(x, y, z, h, c) for x in range(4) for y in range(4) for z in range(2) for h in range(2) for c in range(2)]
+    every = every[1:]
+    random.Random(1).shuffle(every)
+    return sorted(every, key=lambda offset: -far(*offset))
+
+
 def relative_groups():
     every = [(x, y, z) for x in range(4) for y in range(4) for z in range(2)]
     random.Random(0).shuffle(every)
     return [every[i : i + 4] for i in range(0, 32, 4)]
+
+
+def bunch_of(bunches, group):
+    return [group in bunch for bunch in bunches].index(True)
 
 
 def halves(x):
@@ -72,19 +83,15 @@
     cores = [(rcv + d) % 2 for d in range(2)]
     groups = relative_groups()
 
-    def targets(group):
-        x, y, z = group
-        return [
-            (ys[y] * 2 + z_low[z], xs[x] * 4 + z_high[h] * 2 + cores[c])
-            for h in range(2)
-            for c in range(2)
-            if (x, y, z, h, c) != (0, 0, 0, 0, 0)
-        ]
-
-    offsets = [(x, y, z, h, c) for x in range(4) for y in range(4) for z in range(2) for h in range(2) for c in range(2)]
-    offsets = sorted(offsets[1:], key=lambda offset: -far(*offset))
-    everyone = [(ys[y] * 2 + z_low[z], xs[x] * 4 + z_high[h] * 2 + cores[c]) for x, y, z, h, c in offsets]
-    home = [k for k, bunch in enumerate(groups) if (0, 0, 0) in bunch][0]
+    offsets = far_first()
+    order = [offset for bunch in groups for group in bunch for offset in sorted(offsets) if offset[:3] == group]
+
+    def target(offset):
+        x, y, z, h, c = offset
+        return ys[y] * 2 + z_low[z], xs[x] * 4 + z_high[h] * 2 + cores[c]
+
+    everyone = [target(offset) for offset in offsets]
+    home = bunch_of(groups, (0, 0, 0))
 
     def load(b, g):
         rows = pl.ds(b * 4, 4)
@@ -149,17 +156,16 @@
 
     def send(j, h):
         own(j, h).start()
-        for k, bunch in enumerate(groups):
-            for group in bunch:
-                for to in targets(group):
-                    pltpu.make_async_remote_copy(
-                        src_ref=sbuf.at[piece(j, h, to[0] * 16 + to[1])],
-                        dst_ref=rbuf.at[piece(j, h, me)],
-                        send_sem=send_sem.at[j * 2 + h],
-                        recv_sem=recv_sem.at[(j * 2 + h) * 8 + k],
-                        device_id=to,
-                        device_id_type=MESH,
-                    ).start()
+        for offset in order:
+            to, k = target(offset), bunch_of(groups, offset[:3])
+            pltpu.make_async_remote_copy(
+                src_ref=sbuf.at[piece(j, h, to[0] * 16 + to[1])],
+                dst_ref=rbuf.at[piece(j, h, me)],
+                send_sem=send_sem.at[j * 2 + h],
+                recv_sem=recv_sem.at[(j * 2 + h) * 8 + k],
+                device_id=to,
+                device_id_type=MESH,
+            ).start()
 
     def arrival(j, h, k, count):
         return pltpu.make_async_remote_copy(
@@ -205,15 +211,17 @@
     lanes = lax.broadcasted_iota(jnp.int32, (1, 128), 1)
     total = jnp.zeros((1, 128), F32)
 
-    def put(slot, value):
-        high, low = halves(value)
-        rows, columns = slice(slot % 4 * N, slot % 4 * N + N), slice(slot // 4 * N, slot // 4 * N + N)
-        xh[rows, columns] = high
-        xl[rows, columns] = low
-
-    def get(slot):
-        rows, columns = slice(slot % 4 * N, slot % 4 * N + N), slice(slot // 4 * N, slot // 4 * N + N)
-        return xh[rows, columns], xl[rows, columns]
+    def place(slot, rows=slice(0, N)):
+        base = slot % 4 * N
+        return slice(base + rows.start, base + rows.stop), slice(slot // 4 * N, slot // 4 * N + N)
+
+    def put_rows(slot, rows, value):
+        at = place(slot, rows)
+        xh[at], xl[at] = halves(value)
+
+    def get(slot, rows=slice(0, N)):
+        at = place(slot, rows)
+        return xh[at], xl[at]
 
     def model_operands(j):
         for c in range(2):
@@ -299,33 +307,41 @@
         symmetric(1, imag_operands)
 
         cross = -dot3(get(2), get(1))
-        square = dot3(get(3), get(3))
+        high, low = get(3)
+        square = lax.dot_general(high, high, NN, preferred_element_type=F32)
+        mixed = lax.dot_general(high, low, NN, preferred_element_type=F32)
         second = dot3((ah[1], al[1]), get(1))
         flipped = cross.T
-        h_re = 0.5 * (cross + flipped) + 2.0 * square
+        h_re = 0.5 * (cross + flipped) + 2.0 * (square + (mixed + mixed.T))
         h_im = 0.5 * (flipped - cross)
         ah[0], al[0] = halves(h_re)
-        put(7, h_im - h_re)
-        put(0, h_im + h_re)
-        im = whole[1] - (pred[0] + second)
-        resid[1] = im
-        put(6, im)
-        third = dot3((ah[2], al[2]), get(2))
-        re = whole[0] - (pred[0] - third)
-        resid[0] = re
-        put(5, re)
-        put(4, re + im)
-        third = dot3(get(6), get(0))
-        second = dot3(get(5), get(7))
-        first = dot3(get(4), (ah[0], al[0]))
-        re = first - third
-        im = first + second
-        pred[0] = re
-        pred[1] = im
-        numer = jnp.sum(resid[0] * re + resid[1] * im, axis=0, keepdims=True)
-        denom = jnp.sum(re * re + im * im, axis=0, keepdims=True)
+        put_rows(7, slice(0, N), h_im - h_re)
+        put_rows(0, slice(0, N), h_im + h_re)
+        resid[1] = whole[1] - (pred[0] + second)
+        for half in range(2):
+            rows = slice(half * 256, half * 256 + 256)
+            third = dot3((ah[2, rows], al[2, rows]), get(2))
+            re = whole[0, rows] - (pred[0, rows] - third)
+            im = resid[1, rows]
+            resid[0, rows] = re
+            put_rows(4, rows, re + im)
+            put_rows(5, rows, re)
+            put_rows(6, rows, im)
+        sums = []
+        for half in range(2):
+            rows = slice(half * 256, half * 256 + 256)
+            third = dot3(get(6, rows), get(0))
+            second = dot3(get(5, rows), get(7))
+            first = dot3(get(4, rows), (ah[0], al[0]))
+            re = first - third
+            im = first + second
+            pred[0, rows] = re
+            pred[1, rows] = im
+            numer = jnp.sum(resid[0, rows] * re + resid[1, rows] * im, axis=0, keepdims=True)
+            denom = jnp.sum(re * re + im * im, axis=0, keepdims=True)
+            sums.append((numer, denom))
         fold = []
-        for value in (numer, denom):
+        for value in (sums[0][0] + sums[1][0], sums[0][1] + sums[1][1]):
             value = value[:, :128] + value[:, 128:256] + value[:, 256:384] + value[:, 384:]
             fold.append(value + pltpu.roll(value, 64, 1))
         weight = freq_ref[me * 2 + j].astype(F32) * (1.0 / 512)
@@ -424,7 +440,7 @@
         compiler_params=pltpu.CompilerParams(
             collective_id=0, has_side_effects=True, vmem_limit_bytes=44 * 2**20
         ),
-    )(freq_index, traces.reshape(4, 16, 32, samples), primaries.reshape(2, 2, 4, 4, 32, N))
+    )(pltpu.with_memory_space_constraint(freq_index, pltpu.HBM), traces.reshape(4, 16, 32, samples), primaries.reshape(2, 2, 4, 4, 32, N))
     return pl.pallas_call(
         final_kernel,
         out_shape=(big, big),

time: 78.7 us -> 77.6 us (0.986)
  no operation moved by 1% of the time
where the time goes in v4:
time: 77.6 us; the launch traced here: 77.5 us
  Pallas kernels  76.7 us (99%)
  between operations  0.82 us (1%)
    pallas_call x1, Pallas kernels, on_device(): pl.pallas_call(kernel, out_shape=(big, big, jax.ShapeDtypeStruct((8, N),...  73.3 us
    pallas_call x1, Pallas kernels, on_device(): pl.pallas_call(final_kernel, out_shape=(big, big), in_specs=[vmem, vmem,...  3.4 us

profile of v4, /device:TPU:1, one launch (start us, length us, event | category | flops | bytes accessed | tf_op | source)
XLA Modules:
  0.0 77.5 jit_solution(7447439268617598414)
XLA Ops:
  0.6 73.3 %shard_map.50 = (f32[2,2,512,512]{3,2,1,0:T(8,128)S(1)}, f32[2,2,512,512]{3,2,1,0:T(8,128)S(1)}, f32[8,512]{1,0:T(8,128)S(1)}) custom-call(s32[256]{0:T(256)} %freq_hbm.1, f32[4,16,32,1024]{3,2,1,0:T(8,128)} %bitcast.2, f32[2,2,4,4,32,512]{5,4,3,2,1,0:T(8,128)} %bitcast.3), custom_call_target="tpu_custom_call" | custom-call | tf_op jit(solution)/shard_map/pallas_call | solution.py:416
  73.9 3.4 %shard_map.51 = (f32[2,2,512,512]{3,2,1,0:T(8,128)}, f32[2,2,512,512]{3,2,1,0:T(8,128)}) custom-call(f32[2,2,512,512]{3,2,1,0:T(8,128)S(1)} %get-tuple-element.5.resid, f32[2,2,512,512]{3,2,1,0:T(8,128)S(1)} %get-tuple-element.6.pred, f32[8,512]{1,0:T(8,128)S(1)} %get-tuple-element.7.step), custom_call_target="tpu_custom_call" | custom-call | tf_op jit(solution)/shard_map/pallas_call | solution.py:444

commit v5 on v4

--- a/solution.py
+++ b/solution.py
@@ -227,10 +227,8 @@
         for c in range(2):
             prim_copy(j, c).wait()
         model = [raw[4 * c : 4 * c + 4, :, :, j * N : j * N + N].reshape(N, N) for c in range(2)]
-        for index, value in enumerate((model[0] + model[1], model[0], model[1])):
-            high, low = halves(value)
-            ah[index] = high
-            al[index] = low
+        for index, value in enumerate(model):
+            ah[index], al[index] = halves(value)
 
     def assemble(j, h, store):
         for k, bunch in enumerate(groups):
@@ -282,10 +280,19 @@
         put_block(0, rows, columns, value)
 
     def imag_operands(rows, columns, value):
-        real = whole[0, rows, columns]
-        put_block(1, rows, columns, value - real)
-        put_block(2, rows, columns, real + value)
-        put_block(3, rows, columns, value)
+        put_block(1, rows, columns, value)
+
+    def gram(matrix):
+        high, low = matrix
+        square = lax.dot_general(high, high, NN, preferred_element_type=F32)
+        mixed = lax.dot_general(high, low, NN, preferred_element_type=F32)
+        return square + (mixed + mixed.T)
+
+    def real_products():
+        real = get(0)
+        resid[0] = whole[0] - dot3((ah[0], al[0]), real)
+        resid[1] = dot3((ah[1], al[1]), real)
+        pred[0] = gram(real)
 
     for j in range(2):
         model_operands(j)
@@ -296,32 +303,27 @@
                 assemble(0, h, store_both)
 
             symmetric(0, real_operands)
-            pred[0] = dot3((ah[0], al[0]), get(0))
+            real_products()
         else:
             assemble(1, 0, store_part)
             symmetric(0, real_operands)
             for copy in out_copies(resid_out, pred_out, resid, pred, out_sem, 0):
                 copy.wait()
-            pred[0] = dot3((ah[0], al[0]), get(0))
+            real_products()
             assemble(1, 1, store_part)
         symmetric(1, imag_operands)
 
-        cross = -dot3(get(2), get(1))
-        high, low = get(3)
-        square = lax.dot_general(high, high, NN, preferred_element_type=F32)
-        mixed = lax.dot_general(high, low, NN, preferred_element_type=F32)
-        second = dot3((ah[1], al[1]), get(1))
-        flipped = cross.T
-        h_re = 0.5 * (cross + flipped) + 2.0 * (square + (mixed + mixed.T))
-        h_im = 0.5 * (flipped - cross)
-        ah[0], al[0] = halves(h_re)
-        put_rows(7, slice(0, N), h_im - h_re)
-        put_rows(0, slice(0, N), h_im + h_re)
-        resid[1] = whole[1] - (pred[0] + second)
+        imag = get(1)
+        cross = dot3(get(0), imag)
+        h_re = pred[0] + gram(imag)
+        h_im = cross - cross.T
+        put_rows(2, slice(0, N), h_re)
+        put_rows(3, slice(0, N), h_im - h_re)
+        put_rows(7, slice(0, N), h_im + h_re)
+        resid[1] = whole[1] - (resid[1] + dot3((ah[0], al[0]), imag))
         for half in range(2):
             rows = slice(half * 256, half * 256 + 256)
-            third = dot3((ah[2, rows], al[2, rows]), get(2))
-            re = whole[0, rows] - (pred[0, rows] - third)
+            re = resid[0, rows] + dot3((ah[1, rows], al[1, rows]), imag)
             im = resid[1, rows]
             resid[0, rows] = re
             put_rows(4, rows, re + im)
@@ -330,9 +332,9 @@
         sums = []
         for half in range(2):
             rows = slice(half * 256, half * 256 + 256)
-            third = dot3(get(6, rows), get(0))
-            second = dot3(get(5, rows), get(7))
-            first = dot3(get(4, rows), (ah[0], al[0]))
+            third = dot3(get(6, rows), get(7))
+            second = dot3(get(5, rows), get(3))
+            first = dot3(get(4, rows), get(2))
             re = first - third
             im = first + second
             pred[0, rows] = re
@@ -427,8 +429,8 @@
             pltpu.VMEM((4 * DEVICES * 16, 128), F32),
             pltpu.VMEM((4 * DEVICES * 16, 128), F32),
             pltpu.VMEM((2, N, N), F32),
-            pltpu.VMEM((3, N, N), BF16),
-            pltpu.VMEM((3, N, N), BF16),
+            pltpu.VMEM((2, N, N), BF16),
+            pltpu.VMEM((2, N, N), BF16),
             pltpu.VMEM((2, N, N), F32),
             pltpu.VMEM((2, N, N), F32),
             pltpu.SMEM((256,), jnp.int32),

time: 77.6 us -> 77 us (level)
  no operation moved by 1% of the time
where the time goes in v5:
time: 77 us; the launch traced here: 76.8 us
  Pallas kernels  76 us (99%)
  between operations  0.82 us (1%)
    pallas_call x1, Pallas kernels, on_device(): pl.pallas_call(kernel, out_shape=(big, big, jax.ShapeDtypeStruct((8, N),...  72.6 us
    pallas_call x1, Pallas kernels, on_device(): pl.pallas_call(final_kernel, out_shape=(big, big), in_specs=[vmem, vmem,...  3.4 us

profile of v5, /device:TPU:1, one launch (start us, length us, event | category | flops | bytes accessed | tf_op | source)
XLA Modules:
  0.0 76.8 jit_solution(16874514114329391750)
XLA Ops:
  0.6 72.6 %shard_map.50 = (f32[2,2,512,512]{3,2,1,0:T(8,128)S(1)}, f32[2,2,512,512]{3,2,1,0:T(8,128)S(1)}, f32[8,512]{1,0:T(8,128)S(1)}) custom-call(s32[256]{0:T(256)} %freq_hbm.1, f32[4,16,32,1024]{3,2,1,0:T(8,128)} %bitcast.2, f32[2,2,4,4,32,512]{5,4,3,2,1,0:T(8,128)} %bitcast.3), custom_call_target="tpu_custom_call" | custom-call | tf_op jit(solution)/shard_map/pallas_call | solution.py:418
  73.3 3.4 %shard_map.51 = (f32[2,2,512,512]{3,2,1,0:T(8,128)}, f32[2,2,512,512]{3,2,1,0:T(8,128)}) custom-call(f32[2,2,512,512]{3,2,1,0:T(8,128)S(1)} %get-tuple-element.5.resid, f32[2,2,512,512]{3,2,1,0:T(8,128)S(1)} %get-tuple-element.6.pred, f32[8,512]{1,0:T(8,128)S(1)} %get-tuple-element.7.step), custom_call_target="tpu_custom_call" | custom-call | tf_op jit(solution)/shard_map/pallas_call | solution.py:446

commit v6 on v5

--- a/solution.py
+++ b/solution.py
@@ -262,11 +262,12 @@
         for p in range(4):
             for q in range(p, 4):
                 a, b = slice(p * 128, p * 128 + 128), slice(q * 128, q * 128 + 128)
-                value = 0.5 * (whole[c, a, b] + whole[c, b, a].T)
+                first, second = whole[c, a, b], whole[c, b, a]
+                value = 0.5 * (first + second.T)
                 whole[c, a, b] = value
                 then(a, b, value)
                 if p != q:
-                    value = value.T
+                    value = 0.5 * (second + first.T)
                     whole[c, b, a] = value
                     then(b, a, value)
 
@@ -394,18 +395,17 @@
 
 
 def final_kernel(resid, pred, step, resid_out, next_out, new, resid_sem, next_sem):
-    copies = []
-    for j in range(2):
-        for c in range(2):
-            copies.append(pltpu.make_async_copy(resid.at[j, c], resid_out.at[j, c], resid_sem.at[j * 2 + c]))
+    places = [(j, c) for j in range(2) for c in range(2)]
+    copies = [pltpu.make_async_copy(resid.at[at], resid_out.at[at], resid_sem.at[n]) for n, at in enumerate(places)]
+    for copy in copies:
+        copy.start()
+    for n, (j, c) in enumerate(places):
+        for half in range(2):
+            rows = slice(half * 256, half * 256 + 256)
+            new[j, c, rows, :] = resid[j, c, rows, :] - jnp.tile(step[...], (32, 1)) * pred[j, c, rows, :]
+            at = (j, c, pl.ds(half * 256, 256))
+            copies.append(pltpu.make_async_copy(new.at[at], next_out.at[at], next_sem.at[n * 2 + half]))
             copies[-1].start()
-            for half in range(2):
-                rows = slice(half * 256, half * 256 + 256)
-                value = resid[j, c, rows, :] - jnp.tile(step[...], (32, 1)) * pred[j, c, rows, :]
-                new[j, c, rows, :] = value
-                at = (j, c, pl.ds(half * 256, 256))
-                copies.append(pltpu.make_async_copy(new.at[at], next_out.at[at], next_sem.at[j * 4 + c * 2 + half]))
-                copies[-1].start()
     for copy in copies:
         copy.wait()
 

time: 77 us -> 77 us (level)
  no operation moved by 1% of the time
where the time goes in v6:
time: 77 us; the launch traced here: 76.9 us
  Pallas kernels  76 us (99%)
  between operations  0.82 us (1%)
    pallas_call x1, Pallas kernels, on_device(): pl.pallas_call(kernel, out_shape=(big, big, jax.ShapeDtypeStruct((8, N),...  72.6 us
    pallas_call x1, Pallas kernels, on_device(): pl.pallas_call(final_kernel, out_shape=(big, big), in_specs=[vmem, vmem,...  3.4 us

profile of v6, /device:TPU:1, one launch (start us, length us, event | category | flops | bytes accessed | tf_op | source)
XLA Modules:
  0.0 76.9 jit_solution(7442458117615704183)
XLA Ops:
  0.6 72.6 %shard_map.50 = (f32[2,2,512,512]{3,2,1,0:T(8,128)S(1)}, f32[2,2,512,512]{3,2,1,0:T(8,128)S(1)}, f32[8,512]{1,0:T(8,128)S(1)}) custom-call(s32[256]{0:T(256)} %freq_hbm.1, f32[4,16,32,1024]{3,2,1,0:T(8,128)} %bitcast.2, f32[2,2,4,4,32,512]{5,4,3,2,1,0:T(8,128)} %bitcast.3), custom_call_target="tpu_custom_call" | custom-call | tf_op jit(solution)/shard_map/pallas_call | solution.py:418
  73.3 3.4 %shard_map.51 = (f32[2,2,512,512]{3,2,1,0:T(8,128)}, f32[2,2,512,512]{3,2,1,0:T(8,128)}) custom-call(f32[2,2,512,512]{3,2,1,0:T(8,128)S(1)} %get-tuple-element.5.resid, f32[2,2,512,512]{3,2,1,0:T(8,128)S(1)} %get-tuple-element.6.pred, f32[8,512]{1,0:T(8,128)S(1)} %get-tuple-element.7.step), custom_call_target="tpu_custom_call" | custom-call | tf_op jit(solution)/shard_map/pallas_call | solution.py:446
